TPU v7x, 128 devices: a whole 4x4x4 slice. The times are simulated.
128 devices in a mesh: dp: 16 (over z, y), tensor: 8 (over x, core).
Axes of the slice: x: 4, y: 4, z: 4, core: 2. Of those that a mesh axis runs over, the one named last changes fastest.
Arguments:
- dense: bfloat16 [3072, 2048], P('dp'), may hold values from -8 to 8
- bottom_weight: bfloat16 [2048, 16384], P(None, 'tensor'), may hold values from -0.125 to 0.125
- bottom_bias: float32 [16384], P('tensor'), may hold values from -3 to 3
- cross_blocks: bfloat16 [80, 512, 512], P('tensor', 'dp'), may hold values from -0.25 to 0.25
- cross_bias: float32 [16384], P('tensor'), may hold values from -3 to 3
- cotangent: bfloat16 [3072, 16384], P('dp', 'tensor'), may hold values from -6 to 6
- in_blocks: int32 [8, 10], replicated, may hold values from 0 to 31, as said below
- out_blocks: int32 [8, 10], replicated, may hold values from 0 to 31, as said below
- live_slots: int32 [8], replicated, may hold values from 2 to 10, as said below
Outputs:
- cross_out: bfloat16 [3072, 16384], P('dp', 'tensor')
- grad_bottom: float32 [2048, 16384], P('dp', 'tensor')
- grad_bias_bottom: float32 [16384], P('tensor')
- grad_blocks: float32 [80, 512, 512], P('tensor', 'dp')
- grad_bias: float32 [16384], P('tensor')
Inputs may be any that keep to these rules, and one draw needn't show every extreme that they name: `in_blocks`: among the live slots of one tensor device, at most 2 have input blocks held by any one tensor device (blocks s * 16384 / (512 * 8) onward for device s), and this most is reached in every draw. `out_blocks`: among the live slots of one tensor device, at most 2 have output blocks held by any one tensor device, and this most is reached in every draw. `live_slots`: some tensor device has all 10 slots live.
All inputs are finite; a program needn't handle non-finite values.
Results may differ from a plain program's by a relative error of at most 0.014.
Values may be sent and summed in bfloat16 or wider, within the bound.
A program may use at most 128 MiB of HBM per device.

v0:
```python
import jax
import jax.numpy as jnp
from jax import lax
from jax.sharding import PartitionSpec as P

BLK = 512
SLOTS = 10


def slot_ranks(owner, alive):
    order = jnp.arange(owner.shape[1])
    earlier = order[None, :] < order[:, None]
    same = (owner[:, :, None] == owner[:, None, :]) & alive[:, None, :] & earlier[None, :, :]
    return jnp.sum(same.astype(jnp.int32), axis=2)


def post_table(owner_mine, rank_mine, alive_mine, groups, capacity):
    slot_count = owner_mine.shape[0]
    match = (
        (owner_mine[None, None, :] == jnp.arange(groups)[:, None, None])
        & (rank_mine[None, None, :] == jnp.arange(capacity)[None, :, None])
        & alive_mine[None, None, :]
    )
    chosen = jnp.sum(match.astype(jnp.int32) * jnp.arange(slot_count)[None, None, :], axis=2)
    filled = jnp.any(match, axis=2)
    return (chosen, filled)


def pack_parts(parts, chosen, filled):
    picked = jnp.take(parts, chosen.reshape(-1), axis=0) * filled.reshape(-1)[:, None, None].astype(
        parts.dtype
    )
    return picked.reshape(chosen.shape[0], chosen.shape[1] * parts.shape[1], parts.shape[2])


def collect_parts(received, owner, local, rank, alive, target, capacity, per_device):
    groups, span_rows, block_width = received.shape
    row_count = span_rows // capacity
    match = ((owner == target) & alive)[:, :, None] & (
        rank[:, :, None] == jnp.arange(capacity)[None, None, :]
    )
    matches = match[:, :, :, None] & (
        local[:, :, None, None] == jnp.arange(per_device)[None, None, None, :]
    )
    onehot = (
        jnp.sum(matches.astype(jnp.int32), axis=1)
        .reshape(groups * capacity, per_device)
        .astype(jnp.bfloat16)
    )
    flattened = received.reshape(groups * capacity, row_count, block_width)
    summed = jnp.einsum("irb,il->rlb", flattened, onehot, preferred_element_type=jnp.float32)
    return summed.reshape(row_count, per_device * block_width)


def ring_gather(x, axis, n):
    half = x.shape[0] // 2
    right = [(i, (i + 1) % n) for i in range(n)]
    left = [(i, (i - 1) % n) for i in range(n)]
    cur_a, cur_b = (x[:half], x[half:])
    outs_a, outs_b = ([cur_a], [cur_b])
    for _ in range(1, n):
        cur_a = lax.ppermute(cur_a, axis, right)
        cur_b = lax.ppermute(cur_b, axis, left)
        outs_a.append(cur_a)
        outs_b.append(cur_b)
    return (jnp.stack(outs_a), jnp.stack(outs_b))


def take_blocks(stack_a, stack_b, owner, local, me, n):
    steps, half, width = stack_a.shape
    blocks_a = stack_a.reshape(steps, half, width // BLK, BLK)
    blocks_b = stack_b.reshape(steps, half, width // BLK, BLK)
    step_a = (me - owner) % n
    step_b = (owner - me) % n
    top = blocks_a[step_a, :, local, :]
    bottom = blocks_b[step_b, :, local, :]
    return jnp.concatenate([top, bottom], axis=1)


def on_device(
    dense,
    bottom_weight,
    bottom_bias,
    cross_blocks,
    cross_bias,
    cotangent,
    in_blocks,
    out_blocks,
    live_slots,
):
    groups = lax.axis_size("tensor")
    mine = lax.axis_index("tensor")
    row_count = dense.shape[0]
    local_width = bottom_weight.shape[1]
    per_device = local_width // BLK
    capacity = -(-SLOTS // groups)
    preact = jnp.dot(dense, bottom_weight, preferred_element_type=jnp.float32) + bottom_bias
    start = jax.nn.silu(preact).astype(jnp.bfloat16)
    start_wide = start.astype(jnp.float32)
    cot_wide = cotangent.astype(jnp.float32)
    grad_mixed = cot_wide * start_wide
    grad_mixed_low = grad_mixed.astype(jnp.bfloat16)
    alive = jnp.arange(SLOTS)[None, :] < live_slots[:, None]
    alive_mine = alive[mine]
    switch = alive_mine.astype(jnp.bfloat16)[:, None, None]
    in_owner = in_blocks // per_device
    in_local = in_blocks % per_device
    out_owner = out_blocks // per_device
    out_local = out_blocks % per_device
    in_rank = slot_ranks(in_owner, alive)
    out_rank = slot_ranks(out_owner, alive)
    combo = jnp.concatenate([start, grad_mixed_low], axis=1)
    stack_a, stack_b = ring_gather(combo, "tensor", groups)
    fetched = take_blocks(stack_a, stack_b, in_owner[mine], in_local[mine], mine, groups)
    taken = fetched
    product = jnp.einsum(
        "kri,kij->krj",
        taken,
        lax.all_gather(cross_blocks, "dp", axis=1, tiled=True),
        preferred_element_type=jnp.float32,
    )
    parts = product.astype(jnp.bfloat16) * switch
    chosen_out, filled_out = post_table(
        out_owner[mine], out_rank[mine], alive_mine, groups, capacity
    )
    arrived_parts = lax.all_to_all(
        pack_parts(parts, chosen_out, filled_out), "tensor", split_axis=0, concat_axis=0, tiled=True
    )
    mixed = (
        collect_parts(
            arrived_parts, out_owner, out_local, out_rank, alive, mine, capacity, per_device
        )
        + cross_bias
    )
    cross_out = (start_wide * mixed + start_wide).astype(jnp.bfloat16)
    upstream = take_blocks(
        stack_a, stack_b, out_owner[mine], out_local[mine] + per_device, mine, groups
    )
    upstream = upstream * switch
    backward = jnp.einsum(
        "krj,kij->kri",
        upstream,
        lax.all_gather(cross_blocks, "dp", axis=1, tiled=True),
        preferred_element_type=jnp.float32,
    )
    back_parts = backward.astype(jnp.bfloat16)
    chosen_in, filled_in = post_table(in_owner[mine], in_rank[mine], alive_mine, groups, capacity)
    arrived_back = lax.all_to_all(
        pack_parts(back_parts, chosen_in, filled_in),
        "tensor",
        split_axis=0,
        concat_axis=0,
        tiled=True,
    )
    grad_start = collect_parts(
        arrived_back, in_owner, in_local, in_rank, alive, mine, capacity, per_device
    )
    block_terms = jnp.einsum("kri,krj->kij", fetched, upstream, preferred_element_type=jnp.float32)
    grad_blocks = lax.psum_scatter(
        block_terms.astype(jnp.bfloat16), "dp", scatter_dimension=1, tiled=True
    ).astype(jnp.float32)
    grad_start = grad_start + cot_wide * mixed + cot_wide
    sigma = jax.nn.sigmoid(preact)
    grad_pre = grad_start * sigma * (1.0 + preact * (1.0 - sigma))
    grad_pre_low = grad_pre.astype(jnp.bfloat16)
    taken = dense
    grad_bottom = lax.psum_scatter(
        lax.dot_general(
            taken, grad_pre_low, (((0,), (0,)), ((), ())), preferred_element_type=jnp.float32
        ).astype(jnp.bfloat16),
        "dp",
        scatter_dimension=0,
        tiled=True,
    ).astype(jnp.float32)
    bias_sums = lax.psum((jnp.sum(grad_pre, axis=0), jnp.sum(grad_mixed, axis=0)), "dp")
    return (cross_out, grad_bottom, bias_sums[0], grad_blocks, bias_sums[1])


def solution(mesh):
    return jax.shard_map(
        on_device,
        mesh=mesh,
        in_specs=(
            P("dp", None),
            P(None, "tensor"),
            P("tensor"),
            P("tensor", "dp", None),
            P("tensor"),
            P("dp", "tensor"),
            P(),
            P(),
            P(),
        ),
        out_specs=(
            P("dp", "tensor"),
            P("dp", "tensor"),
            P("tensor"),
            P("tensor", "dp", None),
            P("tensor"),
        ),
        check_vma=False,
    )
```

profile of v0, /device:TPU:0, one launch (start us, length us, event | category | flops | bytes accessed | tf_op | source)
XLA Modules:
  0.0 354.9 jit_solution(3943194718781024249)
XLA Ops:
  8.3 7.5 %fusion.8 = (f32[2048]{0:T(1024)}, bf16[192,2048]{1,0:T(8,128)(2,1)S(1)}, f32[192,2048]{1,0:T(8,128)}) fusion(bf16[192,2048]{1,0:T(8,128)(2,1)} %param.16, f32[2048]{0:T(1024)} %param.13, bf16[192,2048]{1,0:T(8,128)(2,1)S(1)} %copy-done, bf16[2048,2048]{1,0:T(8,128)(2,1)} %param.12), kind=kOutput, calls=%fused_computation.30 | convolution fusion | flops 1614542848 | bytes 12337152 | tf_op jit(solution)/shard_map/dot_general | solution.py:97
  19.3 9.8 %collective-permute-done = bf16[96,4096]{1,0:T(8,128)(2,1)} collective-permute-done((bf16[96,4096]{1,0:T(8,128)(2,1)S(1)}, bf16[96,4096]{1,0:T(8,128)(2,1)}, u32[]{:S(2)}, u32[]{:S(2)}) %collective-permute-start) | collective-permute-done | bytes 786464 | tf_op jit(solution)/shard_map/ppermute | solution.py:62
  32.7 9.3 %collective-permute-done.1 = bf16[96,4096]{1,0:T(8,128)(2,1)} collective-permute-done((bf16[96,4096]{1,0:T(8,128)(2,1)}, bf16[96,4096]{1,0:T(8,128)(2,1)}, u32[]{:S(2)}, u32[]{:S(2)}) %collective-permute-start.1) | collective-permute-done | bytes 786464 | tf_op jit(solution)/shard_map/ppermute | solution.py:62
  61.8 6.0 %collective-permute-done.3 = bf16[96,4096]{1,0:T(8,128)(2,1)S(1)} collective-permute-done((bf16[96,4096]{1,0:T(8,128)(2,1)}, bf16[96,4096]{1,0:T(8,128)(2,1)S(1)}, u32[]{:S(2)}, u32[]{:S(2)}) %collective-permute-start.3) | collective-permute-done | bytes 786464 | tf_op jit(solution)/shard_map/ppermute | solution.py:62
  75.4 5.0 %collective-permute-done.4 = bf16[96,4096]{1,0:T(8,128)(2,1)S(1)} collective-permute-done((bf16[96,4096]{1,0:T(8,128)(2,1)S(1)}, bf16[96,4096]{1,0:T(8,128)(2,1)S(1)}, u32[]{:S(2)}, u32[]{:S(2)}) %collective-permute-start.4) | collective-permute-done | bytes 786464 | tf_op jit(solution)/shard_map/ppermute | solution.py:62
  85.2 7.9 %collective-permute-done.5 = bf16[96,4096]{1,0:T(8,128)(2,1)S(1)} collective-permute-done((bf16[96,4096]{1,0:T(8,128)(2,1)S(1)}, bf16[96,4096]{1,0:T(8,128)(2,1)S(1)}, u32[]{:S(2)}, u32[]{:S(2)}) %collective-permute-start.5) | collective-permute-done | bytes 786464 | tf_op jit(solution)/shard_map/ppermute | solution.py:62
  97.8 7.9 %collective-permute-done.6 = bf16[96,4096]{1,0:T(8,128)(2,1)S(1)} collective-permute-done((bf16[96,4096]{1,0:T(8,128)(2,1)S(1)}, bf16[96,4096]{1,0:T(8,128)(2,1)S(1)}, u32[]{:S(2)}, u32[]{:S(2)}) %collective-permute-start.6) | collective-permute-done | bytes 786464 | tf_op jit(solution)/shard_map/ppermute | solution.py:62
  112.6 4.4 %gather_fusion.2 = bf16[10,96,512]{2,1,0:T(8,128)(2,1)} fusion(bf16[8,96,8,512]{3,1,2,0:T(8,128)(2,1)} %copy-done.8, s32[10]{0:T(128)S(1)} %get-tuple-element.52), kind=kCustom, calls=%fused_computation.4 | custom fusion | bytes 1966160 | tf_op jit(solution)/shard_map/gather | solution.py:75
  121.6 4.4 %gather_fusion.3 = bf16[10,96,512]{2,1,0:T(8,128)(2,1)} fusion(bf16[8,96,8,512]{3,1,2,0:T(8,128)(2,1)} %copy_dynamic-update-slice_fusion, s32[10]{0:T(128)S(1)} %get-tuple-element.53), kind=kCustom, calls=%fused_computation.5 | custom fusion | bytes 1966160 | tf_op jit(solution)/shard_map/gather | solution.py:76
  128.1 4.1 %convolution_convert_fusion = bf16[10,512,512]{2,1,0:T(8,128)(2,1)} fusion(bf16[10,192,512]{2,1,0:T(8,128)(2,1)S(1)} %constant_dynamic-update-slice_fusion, bf16[10,96,512]{2,1,0:T(8,128)(2,1)S(1)} %copy-done.10, bf16[10,96,512]{2,1,0:T(8,128)(2,1)S(1)} %copy-done.9, bf16[10]{0:T(256)(128)(2,1)S(1)} %copy-done.19), kind=kOutput, calls=%fused_computation.13 | convolution fusion | flops 1015152640 | bytes 9175060 | tf_op jit(solution)/shard_map/kri,krj->kij/dot_general | solution.py:158
  138.4 4.3 %convert_multiply_fusion.2 = bf16[10,192,512]{2,1,0:T(8,128)(2,1)S(1)} fusion(bf16[10,192,512]{2,1,0:T(8,128)(2,1)} %copy-done.1, bf16[10,512,512]{2,1,0:T(8,128)(2,1)} %all-gather.2.cloned.1.call-done, bf16[10]{0:T(256)(128)(2,1)} %get-tuple-element.45), kind=kOutput, calls=%fused_computation.20 | convolution fusion | flops 1008599040 | bytes 9175060 | tf_op jit(solution)/shard_map/kri,kij->krj/dot_general | solution.py:116
  145.3 3.9 %select_multiply_fusion.1 = bf16[16,192,512]{2,1,0:T(8,128)(2,1)} fusion(bf16[16,192,512]{2,1,0:T(8,128)(2,1)} %gather_fusion.4, pred[16]{0:T(512)(128)(4,1)} %compare_and_fusion.3, bf16[16]{0:T(256)(128)(2,1)} %reshape.558), kind=kLoop, calls=%fused_computation.12 | loop fusion | flops 3145728 | bytes 6291504 | tf_op jit(solution)/shard_map/mul | solution.py:30
  149.2 4.6 %all-to-all-start = ((bf16[8,384,512]{2,1,0:T(8,128)(2,1)}), bf16[8,384,512]{2,1,0:T(8,128)(2,1)}, u32[]{:S(2)}, u32[]{:S(2)}) async-start(bf16[8,384,512]{2,1,0:T(8,128)(2,1)} %bitcast.135), calls=%async_computation | async-start | bytes 6291456 | tf_op jit(solution)/shard_map/all_to_all | solution.py:126
  155.8 5.3 %convolution_convert_fusion.1 = bf16[10,192,512]{2,1,0:T(8,128)(2,1)S(1)} fusion(bf16[10,512,512]{2,1,0:T(8,128)(2,1)} %all-gather.2.cloned.1.call-done, bf16[10,96,512]{2,1,0:T(8,128)(2,1)} %gather_fusion.3, bf16[10,96,512]{2,1,0:T(8,128)(2,1)} %gather_fusion.2, bf16[10]{0:T(256)(128)(2,1)} %get-tuple-element.45), kind=kOutput, calls=%fused_computation.21 | convolution fusion | flops 1013514240 | bytes 9175060 | tf_op jit(solution)/shard_map/krj,kij->kri/dot_general | solution.py:140
  163.7 4.0 %select_multiply_fusion = bf16[16,192,512]{2,1,0:T(8,128)(2,1)} fusion(bf16[16,192,512]{2,1,0:T(8,128)(2,1)} %gather_fusion.5, pred[16]{0:T(512)(128)(4,1)} %compare_and_fusion.2, bf16[16]{0:T(256)(128)(2,1)} %reshape.559), kind=kLoop, calls=%fused_computation.11 | loop fusion | flops 3145728 | bytes 6291504 | tf_op jit(solution)/shard_map/mul | solution.py:30
  167.7 24.5 %all-to-all-done = bf16[8,384,512]{2,1,0:T(8,128)(2,1)} async-done(((bf16[8,384,512]{2,1,0:T(8,128)(2,1)}), bf16[8,384,512]{2,1,0:T(8,128)(2,1)}, u32[]{:S(2)}, u32[]{:S(2)}) %all-to-all-start) | async-done | bytes 3145760 | tf_op jit(solution)/shard_map/all_to_all | solution.py:126
  192.3 4.6 %all-to-all-start.1 = ((bf16[8,384,512]{2,1,0:T(8,128)(2,1)}), bf16[8,384,512]{2,1,0:T(8,128)(2,1)}, u32[]{:S(2)}, u32[]{:S(2)}) async-start(bf16[8,384,512]{2,1,0:T(8,128)(2,1)} %bitcast.134), calls=%async_computation.1 | async-start | bytes 6291456 | tf_op jit(solution)/shard_map/all_to_all | solution.py:148
  197.8 3.8 %fusion.2 = f32[4,192,512]{2,0,1:T(4,128)S(1)} fusion(bf16[16,4,1]{1,0,2:T(8,128)(2,1)S(1)} %bitcast.166, bf16[16,192,512]{2,1,0:T(8,128)(2,1)} %bitcast.10), kind=kOutput, calls=%fused_computation.9 | convolution fusion | flops 12582912 | bytes 4718720 | tf_op jit(solution)/shard_map/irb,il->rlb/dot_general | solution.py:51
  202.2 33.1 %all-to-all-done.1 = bf16[8,384,512]{2,1,0:T(8,128)(2,1)} async-done(((bf16[8,384,512]{2,1,0:T(8,128)(2,1)}), bf16[8,384,512]{2,1,0:T(8,128)(2,1)}, u32[]{:S(2)}, u32[]{:S(2)}) %all-to-all-start.1) | async-done | bytes 3145760 | tf_op jit(solution)/shard_map/all_to_all | solution.py:148
  235.3 4.0 %fusion = f32[4,192,512]{2,0,1:T(4,128)S(1)} fusion(bf16[16,4,1]{1,0,2:T(8,128)(2,1)S(1)} %bitcast.167, bf16[16,192,512]{2,1,0:T(8,128)(2,1)} %bitcast.22), kind=kOutput, calls=%fused_computation.7 | convolution fusion | flops 12582912 | bytes 4718720 | tf_op jit(solution)/shard_map/irb,il->rlb/dot_general | solution.py:51
  241.8 5.6 %convert_bitcast_fusion = bf16[2048,2048]{0,1:T(8,128)(2,1)} fusion(bf16[192,2048]{1,0:T(8,128)(2,1)S(1)} %copy-done, bf16[192,2048]{1,0:T(8,128)(2,1)S(1)} %get-tuple-element.42), kind=kOutput, calls=%fused_computation.6 | convolution fusion | flops 1614807040 | bytes 9961472 | tf_op jit(solution)/shard_map/dot_general | solution.py:168
  247.4 12.4 %copy.125 = bf16[2048,2048]{1,0:T(8,128)(2,1)} copy(bf16[2048,2048]{0,1:T(8,128)(2,1)} %convert_bitcast_fusion) | data formatting | bytes 16777216
  260.5 76.5 %all-reduce = (f32[2048]{0:T(1024)}, f32[2048]{0:T(1024)}) all-reduce(f32[2048]{0:T(1024)S(1)} %get-tuple-element.41, f32[2048]{0:T(1024)S(1)} %copy-done.20), channel_id=1, replica_groups=mesh['dp'=16,'tensor'=8] {'dp'}, use_global_device_ids=true, to_apply=%region_10.12 | all-reduce | flops 4096 | bytes 32768 | tf_op jit(solution)/shard_map/psum | solution.py:175
  338.9 7.0 %reduce-scatter.7.cloned.1.call-done = bf16[128,2048]{1,0:T(8,128)(2,1)} async-done(((bf16[2048,2048]{1,0:T(8,128)(2,1)}), bf16[128,2048]{1,0:T(8,128)(2,1)}) %reduce-scatter.7.cloned.1.call-update) | async-done | bytes 524304
  (180 shorter events, 80.7 us)
Async XLA Ops:
  7.2 131.2 %all-gather.2.cloned.1.call-start = ((), (), s32[]{:S(2)}) async-start(), calls=%async_computation.4 | async-start | bytes 5570560 | tf_op jit(solution)/shard_map/all_gather | solution.py:119
  7.9 329.0 %reduce-scatter.5.cloned.1.call-start = ((), (), s32[]{:S(2)}) async-start(), calls=%async_computation.5 | async-start | bytes 5570560 | tf_op jit(solution)/shard_map/reduce_scatter | solution.py:159
  16.3 28.7 %copy-start.3 = (bf16[96,4096]{1,0:T(8,128)(2,1)}, bf16[96,4096]{1,0:T(8,128)(2,1)S(1)}, u32[]{:S(2)}) copy-start(bf16[96,4096]{1,0:T(8,128)(2,1)S(1)} %get-tuple-element.51) | copy-start | bytes 2359300
  16.3 30.1 %copy-start.2 = (bf16[96,4096]{1,0:T(8,128)(2,1)}, bf16[96,4096]{1,0:T(8,128)(2,1)S(1)}, u32[]{:S(2)}) copy-start(bf16[96,4096]{1,0:T(8,128)(2,1)S(1)} %get-tuple-element.50) | copy-start | bytes 2359300
  16.3 12.7 %collective-permute-start = (bf16[96,4096]{1,0:T(8,128)(2,1)S(1)}, bf16[96,4096]{1,0:T(8,128)(2,1)}, u32[]{:S(2)}, u32[]{:S(2)}) collective-permute-start(bf16[96,4096]{1,0:T(8,128)(2,1)S(1)} %get-tuple-element.51), channel_id=1, source_target_pairs={{0,1},{1,2},{2,3},{3,4},{4,5},{5,6},{6,7},{7,0},{8,9},{9,10},{10,1... | collective-permute-start | bytes 2359304 | tf_op jit(solution)/shard_map/ppermute | solution.py:62
  16.3 12.7 %collective-permute-start.7 = (bf16[96,4096]{1,0:T(8,128)(2,1)S(1)}, bf16[96,4096]{1,0:T(8,128)(2,1)}, u32[]{:S(2)}, u32[]{:S(2)}) collective-permute-start(bf16[96,4096]{1,0:T(8,128)(2,1)S(1)} %get-tuple-element.50), channel_id=1, source_target_pairs={{0,7},{1,0},{2,1},{3,2},{4,3},{5,4},{6,5},{7,6},{8,15},{9,8},{10,9... | collective-permute-start | bytes 2359304 | tf_op jit(solution)/shard_map/ppermute | solution.py:63
  29.1 12.9 %collective-permute-start.1 = (bf16[96,4096]{1,0:T(8,128)(2,1)}, bf16[96,4096]{1,0:T(8,128)(2,1)}, u32[]{:S(2)}, u32[]{:S(2)}) collective-permute-start(bf16[96,4096]{1,0:T(8,128)(2,1)} %collective-permute-done), channel_id=1, source_target_pairs={{0,1},{1,2},{2,3},{3,4},{4,5},{5,6},{6,7},{7,0},{8,9},{9,10},{10,1... | collective-permute-start | bytes 2359304 | tf_op jit(solution)/shard_map/ppermute | solution.py:62
  29.1 12.9 %collective-permute-start.8 = (bf16[96,4096]{1,0:T(8,128)(2,1)}, bf16[96,4096]{1,0:T(8,128)(2,1)}, u32[]{:S(2)}, u32[]{:S(2)}) collective-permute-start(bf16[96,4096]{1,0:T(8,128)(2,1)} %collective-permute-done.7), channel_id=1, source_target_pairs={{0,7},{1,0},{2,1},{3,2},{4,3},{5,4},{6,5},{7,6},{8,15},{9,8},{10,9... | collective-permute-start | bytes 2359304 | tf_op jit(solution)/shard_map/ppermute | solution.py:63
  32.1 16.9 %copy-start.13 = (s32[8,10]{1,0:T(8,128)}, s32[8,10]{1,0:T(8,128)S(1)}, u32[]{:S(2)}) copy-start(s32[8,10]{1,0:T(8,128)S(1)} %add_select_fusion) | copy-start | bytes 964
  32.7 99.4 %copy-start.12 = (s32[8,10]{1,0:T(8,128)}, s32[8,10]{1,0:T(8,128)S(1)}, u32[]{:S(2)}) copy-start(s32[8,10]{1,0:T(8,128)S(1)} %get-tuple-element.57) | copy-start | bytes 964
  32.7 99.5 %copy-start.11 = (s32[8,10]{1,0:T(8,128)}, s32[8,10]{1,0:T(8,128)S(1)}, u32[]{:S(2)}) copy-start(s32[8,10]{1,0:T(8,128)S(1)} %get-tuple-element.48) | copy-start | bytes 964
  42.0 12.9 %collective-permute-start.2 = (bf16[96,4096]{1,0:T(8,128)(2,1)}, bf16[96,4096]{1,0:T(8,128)(2,1)}, u32[]{:S(2)}, u32[]{:S(2)}) collective-permute-start(bf16[96,4096]{1,0:T(8,128)(2,1)} %collective-permute-done.1), channel_id=1, source_target_pairs={{0,1},{1,2},{2,3},{3,4},{4,5},{5,6},{6,7},{7,0},{8,9},{9,10},{10,1... | collective-permute-start | bytes 2359304 | tf_op jit(solution)/shard_map/ppermute | solution.py:62
  42.0 12.9 %collective-permute-start.9 = (bf16[96,4096]{1,0:T(8,128)(2,1)}, bf16[96,4096]{1,0:T(8,128)(2,1)}, u32[]{:S(2)}, u32[]{:S(2)}) collective-permute-start(bf16[96,4096]{1,0:T(8,128)(2,1)} %collective-permute-done.8), channel_id=1, source_target_pairs={{0,7},{1,0},{2,1},{3,2},{4,3},{5,4},{6,5},{7,6},{8,15},{9,8},{10,9... | collective-permute-start | bytes 2359304 | tf_op jit(solution)/shard_map/ppermute | solution.py:63
  54.9 12.8 %collective-permute-start.3 = (bf16[96,4096]{1,0:T(8,128)(2,1)}, bf16[96,4096]{1,0:T(8,128)(2,1)S(1)}, u32[]{:S(2)}, u32[]{:S(2)}) collective-permute-start(bf16[96,4096]{1,0:T(8,128)(2,1)} %collective-permute-done.2), channel_id=1, source_target_pairs={{0,1},{1,2},{2,3},{3,4},{4,5},{5,6},{6,7},{7,0},{8,9},{9,10},{10,1... | collective-permute-start | bytes 2359304 | tf_op jit(solution)/shard_map/ppermute | solution.py:62
  55.0 13.1 %collective-permute-start.10 = (bf16[96,4096]{1,0:T(8,128)(2,1)}, bf16[96,4096]{1,0:T(8,128)(2,1)S(1)}, u32[]{:S(2)}, u32[]{:S(2)}) collective-permute-start(bf16[96,4096]{1,0:T(8,128)(2,1)} %collective-permute-done.9), channel_id=1, source_target_pairs={{0,7},{1,0},{2,1},{3,2},{4,3},{5,4},{6,5},{7,6},{8,15},{9,8},{10,9... | collective-permute-start | bytes 2359304 | tf_op jit(solution)/shard_map/ppermute | solution.py:63
  67.8 12.6 %collective-permute-start.4 = (bf16[96,4096]{1,0:T(8,128)(2,1)S(1)}, bf16[96,4096]{1,0:T(8,128)(2,1)S(1)}, u32[]{:S(2)}, u32[]{:S(2)}) collective-permute-start(bf16[96,4096]{1,0:T(8,128)(2,1)S(1)} %collective-permute-done.3), channel_id=1, source_target_pairs={{0,1},{1,2},{2,3},{3,4},{4,5},{5,6},{6,7},{7,0},{8,9},{9,10},{10,1... | collective-permute-start | bytes 2359304 | tf_op jit(solution)/shard_map/ppermute | solution.py:62
  68.0 12.7 %collective-permute-start.11 = (bf16[96,4096]{1,0:T(8,128)(2,1)S(1)}, bf16[96,4096]{1,0:T(8,128)(2,1)S(1)}, u32[]{:S(2)}, u32[]{:S(2)}) collective-permute-start(bf16[96,4096]{1,0:T(8,128)(2,1)S(1)} %collective-permute-done.10), channel_id=1, source_target_pairs={{0,7},{1,0},{2,1},{3,2},{4,3},{5,4},{6,5},{7,6},{8,15},{9,8},{10,9... | collective-permute-start | bytes 2359304 | tf_op jit(solution)/shard_map/ppermute | solution.py:63
  80.4 12.6 %collective-permute-start.5 = (bf16[96,4096]{1,0:T(8,128)(2,1)S(1)}, bf16[96,4096]{1,0:T(8,128)(2,1)S(1)}, u32[]{:S(2)}, u32[]{:S(2)}) collective-permute-start(bf16[96,4096]{1,0:T(8,128)(2,1)S(1)} %collective-permute-done.4), channel_id=1, source_target_pairs={{0,1},{1,2},{2,3},{3,4},{4,5},{5,6},{6,7},{7,0},{8,9},{9,10},{10,1... | collective-permute-start | bytes 2359304 | tf_op jit(solution)/shard_map/ppermute | solution.py:62
  80.8 12.6 %collective-permute-start.12 = (bf16[96,4096]{1,0:T(8,128)(2,1)S(1)}, bf16[96,4096]{1,0:T(8,128)(2,1)S(1)}, u32[]{:S(2)}, u32[]{:S(2)}) collective-permute-start(bf16[96,4096]{1,0:T(8,128)(2,1)S(1)} %collective-permute-done.11), channel_id=1, source_target_pairs={{0,7},{1,0},{2,1},{3,2},{4,3},{5,4},{6,5},{7,6},{8,15},{9,8},{10,9... | collective-permute-start | bytes 2359304 | tf_op jit(solution)/shard_map/ppermute | solution.py:63
  93.0 12.6 %collective-permute-start.6 = (bf16[96,4096]{1,0:T(8,128)(2,1)S(1)}, bf16[96,4096]{1,0:T(8,128)(2,1)S(1)}, u32[]{:S(2)}, u32[]{:S(2)}) collective-permute-start(bf16[96,4096]{1,0:T(8,128)(2,1)S(1)} %collective-permute-done.5), channel_id=1, source_target_pairs={{0,1},{1,2},{2,3},{3,4},{4,5},{5,6},{6,7},{7,0},{8,9},{9,10},{10,1... | collective-permute-start | bytes 2359304 | tf_op jit(solution)/shard_map/ppermute | solution.py:62
  93.4 12.6 %collective-permute-start.13 = (bf16[96,4096]{1,0:T(8,128)(2,1)S(1)}, bf16[96,4096]{1,0:T(8,128)(2,1)S(1)}, u32[]{:S(2)}, u32[]{:S(2)}) collective-permute-start(bf16[96,4096]{1,0:T(8,128)(2,1)S(1)} %collective-permute-done.12), channel_id=1, source_target_pairs={{0,7},{1,0},{2,1},{3,2},{4,3},{5,4},{6,5},{7,6},{8,15},{9,8},{10,9... | collective-permute-start | bytes 2359304 | tf_op jit(solution)/shard_map/ppermute | solution.py:63
  149.2 43.1 %all-to-all-start = ((bf16[8,384,512]{2,1,0:T(8,128)(2,1)}), bf16[8,384,512]{2,1,0:T(8,128)(2,1)}, u32[]{:S(2)}, u32[]{:S(2)}) async-start(bf16[8,384,512]{2,1,0:T(8,128)(2,1)} %bitcast.135), calls=%async_computation | async-start | bytes 6291456 | tf_op jit(solution)/shard_map/all_to_all | solution.py:126
  192.3 43.0 %all-to-all-start.1 = ((bf16[8,384,512]{2,1,0:T(8,128)(2,1)}), bf16[8,384,512]{2,1,0:T(8,128)(2,1)}, u32[]{:S(2)}, u32[]{:S(2)}) async-start(bf16[8,384,512]{2,1,0:T(8,128)(2,1)} %bitcast.134), calls=%async_computation.1 | async-start | bytes 6291456 | tf_op jit(solution)/shard_map/all_to_all | solution.py:148
  196.9 149.0 %reduce-scatter.7.cloned.1.call-start = ((), (), s32[]{:S(2)}) async-start(), calls=%async_computation.6 | async-start | bytes 8912896
  (25 other events, 147.1 us)
Sparse Core Ops, SparseCore 0:
  10.2 58.9 all-gather.1
  132.3 81.9 reduce-scatter.4
  259.9 85.9 reduce-scatter.6
where the time goes:
time: 356 us; the launch traced here: 355 us
  waiting for transfers between devices  115 us (32%)
  blocking collectives  76.5 us (21%)
  local copies, waits for them, and re-layouts  64.5 us (18%)
  matrix products  34.6 us (10%)
  starting transfers between devices  30.9 us (9%)
  other arithmetic  18.7 us (5%)
  between operations  14.3 us (4%)
    psum x1, blocking collectives, on_device(): lax.psum((jnp.sum(grad_pre, axis=0), jnp.sum(grad_mixed, axis=0)), 'dp')  76.5 us
    ppermute x7, waiting for transfers between devices, ring_gather(): cur_a = lax.ppermute(cur_a, axis, right)  49 us
    unnamed x96, local copies, waits for them, and re-layouts  38.9 us
    all_to_all x1, waiting for transfers between devices, on_device(): lax.all_to_all(pack_parts(back_parts, chosen_in, filled_in), 'tensor', sp...  33.1 us
    all_to_all x1, waiting for transfers between devices, on_device(): lax.all_to_all(pack_parts(parts, chosen_out, filled_out), 'tensor', split...  24.5 us
    ppermute x7, starting transfers between devices, ring_gather(): cur_b = lax.ppermute(cur_b, axis, left)  21.6 us
    mul x2, other arithmetic, pack_parts(): jnp.take(parts, chosen.reshape(-1), axis=0)  7.95 us
    gather x2, local copies, waits for them, and re-layouts, take_blocks(): top = blocks_a[step_a, :, local, :]  7.85 us
  transfers between devices with their start and end apart: 19, of which 14 were waited for; matrix products, arithmetic and copies ran while one was open for 31% of the time, Pallas kernels for 0%

commit v1 on v0

--- a/solution.py
+++ b/solution.py
@@ -5,6 +5,17 @@
 
 BLK = 512
 SLOTS = 10
+
+
+def split_up(shard, dim, size):
+    before, after = (shard.shape[:dim], shard.shape[dim + 1 :])
+    return jnp.moveaxis(shard.reshape(*before, size, -1, *after), dim, 0)
+
+
+def laid_out(blocks, dim):
+    blocks = jnp.moveaxis(blocks, 0, dim)
+    lengths = blocks.shape
+    return blocks.reshape(*lengths[:dim], lengths[dim] * lengths[dim + 1], *lengths[dim + 2 :])
 
 
 def slot_ranks(owner, alive):
@@ -145,13 +156,15 @@
     )
     back_parts = backward.astype(jnp.bfloat16)
     chosen_in, filled_in = post_table(in_owner[mine], in_rank[mine], alive_mine, groups, capacity)
-    arrived_back = lax.all_to_all(
-        pack_parts(back_parts, chosen_in, filled_in),
-        "tensor",
-        split_axis=0,
-        concat_axis=0,
-        tiled=True,
-    )
+    x_2 = pack_parts(back_parts, chosen_in, filled_in)
+    peers, here = (lax.axis_size("tensor"), lax.axis_index("tensor"))
+    blocks = split_up(x_2, 0, peers)
+    outs = [blocks[here]]
+    for hop in range(1, peers):
+        sent = blocks[here ^ hop]
+        outs.append(lax.ppermute(sent, "tensor", [(i_2, i_2 ^ hop) for i_2 in range(peers)]))
+    blocks = jnp.stack(outs)[here ^ jnp.arange(peers)]
+    arrived_back = laid_out(blocks, 0)
     grad_start = collect_parts(
         arrived_back, in_owner, in_local, in_rank, alive, mine, capacity, per_device
     )

time: 356 us -> 359 us (level)
  local copies, waits for them, and re-layouts: 64.5 us -> 70.6 us
  starting transfers between devices: 30.9 us -> 36.3 us
  waiting for transfers between devices: 115 us -> 111 us
  other arithmetic: 18.7 us -> 14.8 us
    ppermute x0 -> x7, waiting for transfers between devices: none -> 48.3 us  [on_device(): lax.ppermute(sent, 'tensor', [(i_2, i_2 ^ hop) for i_2 in range(peers)])]
    all_to_all x1 -> x0, waiting for transfers between devices: 33.1 us -> none  [on_device(): lax.all_to_all(pack_parts(back_parts, chosen_in, filled_in), 'tensor', sp...]
    all_to_all x1, waiting for transfers between devices: 24.5 us -> 0.01 us  [on_device(): lax.all_to_all(pack_parts(parts, chosen_out, filled_out), 'tensor', split...]
    ppermute x0 -> x7, starting transfers between devices: none -> 9.57 us  [on_device(): lax.ppermute(sent, 'tensor', [(i_2, i_2 ^ hop) for i_2 in range(peers)])]
    all_to_all x1 -> x0, starting transfers between devices: 4.57 us -> none  [on_device(): lax.all_to_all(pack_parts(back_parts, chosen_in, filled_in), 'tensor', sp...]
    gather x0 -> x1, local copies, waits for them, and re-layouts: none -> 4.35 us  [on_device(): blocks = jnp.stack(outs)[here ^ jnp.arange(peers)]]
  transfers between devices with their start and end apart: 19 -> 25, of which waited for: 14 -> 17; matrix products, arithmetic and copies ran while one was open for 31% -> 31% of each run, Pallas kernels for 0% -> 0%
where the time goes in v1:
time: 359 us; the launch traced here: 358 us
  waiting for transfers between devices  111 us (31%)
  blocking collectives  76.5 us (21%)
  local copies, waits for them, and re-layouts  70.6 us (20%)
  starting transfers between devices  36.3 us (10%)
  matrix products  34.4 us (10%)
  other arithmetic  14.8 us (4%)
  between operations  14.4 us (4%)
    psum x1, blocking collectives, on_device(): lax.psum((jnp.sum(grad_pre, axis=0), jnp.sum(grad_mixed, axis=0)), 'dp')  76.5 us
    ppermute x7, waiting for transfers between devices, ring_gather(): cur_a = lax.ppermute(cur_a, axis, right)  52.2 us
    ppermute x7, waiting for transfers between devices, on_device(): lax.ppermute(sent, 'tensor', [(i_2, i_2 ^ hop) for i_2 in range(peers)])  48.3 us
    unnamed x96, local copies, waits for them, and re-layouts  39.3 us
    ppermute x7, starting transfers between devices, ring_gather(): cur_b = lax.ppermute(cur_b, axis, left)  22 us
    ppermute x7, starting transfers between devices, on_device(): lax.ppermute(sent, 'tensor', [(i_2, i_2 ^ hop) for i_2 in range(peers)])  9.57 us
    unnamed x4, waiting for transfers between devices  8.39 us
    dot_general x2, matrix products, collect_parts(): jnp.einsum('irb,il->rlb', flattened, onehot, preferred_element_type=jnp.f...  7.79 us
  transfers between devices with their start and end apart: 25, of which 17 were waited for; matrix products, arithmetic and copies ran while one was open for 31% of the time, Pallas kernels for 0%

profile of v1, /device:TPU:0, one launch (start us, length us, event | category | flops | bytes accessed | tf_op | source)
XLA Modules:
  0.0 357.8 jit_solution(3610568920145188674)
XLA Ops:
  8.3 7.6 %fusion.8 = (f32[2048]{0:T(1024)}, bf16[192,2048]{1,0:T(8,128)(2,1)S(1)}, f32[192,2048]{1,0:T(8,128)}) fusion(bf16[192,2048]{1,0:T(8,128)(2,1)} %param.16, f32[2048]{0:T(1024)} %param.13, bf16[192,2048]{1,0:T(8,128)(2,1)S(1)} %copy-done, bf16[2048,2048]{1,0:T(8,128)(2,1)} %param.12), kind=kOutput, calls=%fused_computation.31 | convolution fusion | flops 1614542848 | bytes 12337152 | tf_op jit(solution)/shard_map/dot_general | solution.py:108
  19.3 9.8 %collective-permute-done = bf16[96,4096]{1,0:T(8,128)(2,1)} collective-permute-done((bf16[96,4096]{1,0:T(8,128)(2,1)S(1)}, bf16[96,4096]{1,0:T(8,128)(2,1)}, u32[]{:S(2)}, u32[]{:S(2)}) %collective-permute-start) | collective-permute-done | bytes 786464 | tf_op jit(solution)/shard_map/ppermute | solution.py:73
  32.7 9.3 %collective-permute-done.1 = bf16[96,4096]{1,0:T(8,128)(2,1)} collective-permute-done((bf16[96,4096]{1,0:T(8,128)(2,1)}, bf16[96,4096]{1,0:T(8,128)(2,1)}, u32[]{:S(2)}, u32[]{:S(2)}) %collective-permute-start.1) | collective-permute-done | bytes 786464 | tf_op jit(solution)/shard_map/ppermute | solution.py:73
  49.5 5.3 %collective-permute-done.2 = bf16[96,4096]{1,0:T(8,128)(2,1)S(1)} collective-permute-done((bf16[96,4096]{1,0:T(8,128)(2,1)}, bf16[96,4096]{1,0:T(8,128)(2,1)S(1)}, u32[]{:S(2)}, u32[]{:S(2)}) %collective-permute-start.2) | collective-permute-done | bytes 786464 | tf_op jit(solution)/shard_map/ppermute | solution.py:73
  61.7 5.7 %collective-permute-done.3 = bf16[96,4096]{1,0:T(8,128)(2,1)S(1)} collective-permute-done((bf16[96,4096]{1,0:T(8,128)(2,1)S(1)}, bf16[96,4096]{1,0:T(8,128)(2,1)S(1)}, u32[]{:S(2)}, u32[]{:S(2)}) %collective-permute-start.3) | collective-permute-done | bytes 786464 | tf_op jit(solution)/shard_map/ppermute | solution.py:73
  73.1 7.0 %collective-permute-done.4 = bf16[96,4096]{1,0:T(8,128)(2,1)S(1)} collective-permute-done((bf16[96,4096]{1,0:T(8,128)(2,1)S(1)}, bf16[96,4096]{1,0:T(8,128)(2,1)S(1)}, u32[]{:S(2)}, u32[]{:S(2)}) %collective-permute-start.4) | collective-permute-done | bytes 786464 | tf_op jit(solution)/shard_map/ppermute | solution.py:73
  85.1 7.6 %collective-permute-done.5 = bf16[96,4096]{1,0:T(8,128)(2,1)S(1)} collective-permute-done((bf16[96,4096]{1,0:T(8,128)(2,1)S(1)}, bf16[96,4096]{1,0:T(8,128)(2,1)S(1)}, u32[]{:S(2)}, u32[]{:S(2)}) %collective-permute-start.5) | collective-permute-done | bytes 786464 | tf_op jit(solution)/shard_map/ppermute | solution.py:73
  97.8 7.6 %collective-permute-done.6 = bf16[96,4096]{1,0:T(8,128)(2,1)S(1)} collective-permute-done((bf16[96,4096]{1,0:T(8,128)(2,1)S(1)}, bf16[96,4096]{1,0:T(8,128)(2,1)S(1)}, u32[]{:S(2)}, u32[]{:S(2)}) %collective-permute-start.6) | collective-permute-done | bytes 786464 | tf_op jit(solution)/shard_map/ppermute | solution.py:73
  112.5 4.4 %gather_fusion.2 = bf16[10,96,512]{2,1,0:T(8,128)(2,1)} fusion(bf16[8,96,8,512]{3,1,2,0:T(8,128)(2,1)} %copy-done.6, s32[10]{0:T(128)S(1)} %get-tuple-element.60), kind=kCustom, calls=%fused_computation.4 | custom fusion | bytes 1966160 | tf_op jit(solution)/shard_map/gather | solution.py:86
  121.5 4.4 %gather_fusion.3 = bf16[10,96,512]{2,1,0:T(8,128)(2,1)} fusion(bf16[8,96,8,512]{3,1,2,0:T(8,128)(2,1)} %copy_dynamic-update-slice_fusion, s32[10]{0:T(128)S(1)} %get-tuple-element.61), kind=kCustom, calls=%fused_computation.5 | custom fusion | bytes 1966160 | tf_op jit(solution)/shard_map/gather | solution.py:87
  128.1 4.1 %convolution_convert_fusion = bf16[10,512,512]{2,1,0:T(8,128)(2,1)} fusion(bf16[10,192,512]{2,1,0:T(8,128)(2,1)S(1)} %constant_dynamic-update-slice_fusion, bf16[10,96,512]{2,1,0:T(8,128)(2,1)S(1)} %copy-done.8, bf16[10,96,512]{2,1,0:T(8,128)(2,1)S(1)} %copy-done.7, bf16[10]{0:T(256)(128)(2,1)S(1)} %copy-done.15), kind=kOutput, calls=%fused_computation.14 | convolution fusion | flops 1015152640 | bytes 9175060 | tf_op jit(solution)/shard_map/kri,krj->kij/dot_general | solution.py:171
  137.8 4.3 %convert_multiply_fusion.2 = bf16[10,192,512]{2,1,0:T(8,128)(2,1)S(1)} fusion(bf16[10,192,512]{2,1,0:T(8,128)(2,1)} %copy-done.1, bf16[10,512,512]{2,1,0:T(8,128)(2,1)} %all-gather.2.cloned.1.call-done, bf16[10]{0:T(256)(128)(2,1)} %get-tuple-element.45), kind=kOutput, calls=%fused_computation.21 | convolution fusion | flops 1008599040 | bytes 9175060 | tf_op jit(solution)/shard_map/kri,kij->krj/dot_general | solution.py:127
  148.5 4.6 %all-to-all-start = ((bf16[8,384,512]{2,1,0:T(8,128)(2,1)}), bf16[8,384,512]{2,1,0:T(8,128)(2,1)}, u32[]{:S(2)}, u32[]{:S(2)}) async-start(bf16[8,384,512]{2,1,0:T(8,128)(2,1)} %bitcast.163), calls=%async_computation | async-start | bytes 6291456 | tf_op jit(solution)/shard_map/all_to_all | solution.py:137
  153.2 5.1 %convolution_convert_fusion.1 = bf16[10,192,512]{2,1,0:T(8,128)(2,1)S(1)} fusion(bf16[10,512,512]{2,1,0:T(8,128)(2,1)} %all-gather.2.cloned.1.call-done, bf16[10,96,512]{2,1,0:T(8,128)(2,1)} %gather_fusion.3, bf16[10,96,512]{2,1,0:T(8,128)(2,1)} %gather_fusion.2, bf16[10]{0:T(256)(128)(2,1)S(1)} %copy-done.16), kind=kOutput, calls=%fused_computation.22 | convolution fusion | flops 1013514240 | bytes 9175060 | tf_op jit(solution)/shard_map/krj,kij->kri/dot_general | solution.py:151
  174.9 24.0 %collective-permute-done.15 = bf16[1,384,512]{2,1,0:T(8,128)(2,1)S(1)} collective-permute-done((bf16[1,384,512]{2,1,0:T(8,128)(2,1)}, bf16[1,384,512]{2,1,0:T(8,128)(2,1)S(1)}, u32[]{:S(2)}, u32[]{:S(2)}) %collective-permute-start.15) | collective-permute-done | bytes 393248 | tf_op jit(solution)/shard_map/ppermute | solution.py:165
  200.5 5.8 %collective-permute-done.16 = bf16[1,384,512]{2,1,0:T(8,128)(2,1)S(1)} collective-permute-done((bf16[1,384,512]{2,1,0:T(8,128)(2,1)}, bf16[1,384,512]{2,1,0:T(8,128)(2,1)S(1)}, u32[]{:S(2)}, u32[]{:S(2)}) %collective-permute-start.16) | collective-permute-done | bytes 393248 | tf_op jit(solution)/shard_map/ppermute | solution.py:165
  207.2 10.2 %collective-permute-done.17 = bf16[1,384,512]{2,1,0:T(8,128)(2,1)S(1)} collective-permute-done((bf16[1,384,512]{2,1,0:T(8,128)(2,1)}, bf16[1,384,512]{2,1,0:T(8,128)(2,1)S(1)}, u32[]{:S(2)}, u32[]{:S(2)}) %collective-permute-start.17) | collective-permute-done | bytes 393248 | tf_op jit(solution)/shard_map/ppermute | solution.py:165
  218.1 6.7 %collective-permute-done.18 = bf16[1,384,512]{2,1,0:T(8,128)(2,1)S(1)} collective-permute-done((bf16[1,384,512]{2,1,0:T(8,128)(2,1)}, bf16[1,384,512]{2,1,0:T(8,128)(2,1)S(1)}, u32[]{:S(2)}, u32[]{:S(2)}) %collective-permute-start.18) | collective-permute-done | bytes 393248 | tf_op jit(solution)/shard_map/ppermute | solution.py:165
  228.8 4.3 %gather_fusion.4 = bf16[8,384,512]{2,1,0:T(8,128)(2,1)} fusion(bf16[8,384,512]{2,1,0:T(8,128)(2,1)} %bitcast.170, s32[1024]{0:T(1024)S(1)} %pad_clamp_fusion), kind=kCustom, calls=%fused_computation.6 | custom fusion | bytes 6291488 | tf_op jit(solution)/shard_map/gather | solution.py:166
  237.6 4.0 %fusion.2 = f32[4,192,512]{2,0,1:T(4,128)S(1)} fusion(bf16[16,4,1]{1,0,2:T(8,128)(2,1)S(1)} %bitcast.199, bf16[16,192,512]{2,1,0:T(8,128)(2,1)} %bitcast.10), kind=kOutput, calls=%fused_computation.10 | convolution fusion | flops 12582912 | bytes 4718720 | tf_op jit(solution)/shard_map/irb,il->rlb/dot_general | solution.py:62
  244.1 5.6 %convert_bitcast_fusion = bf16[2048,2048]{0,1:T(8,128)(2,1)} fusion(bf16[192,2048]{1,0:T(8,128)(2,1)S(1)} %copy-done, bf16[192,2048]{1,0:T(8,128)(2,1)S(1)} %get-tuple-element.42), kind=kOutput, calls=%fused_computation.7 | convolution fusion | flops 1614807040 | bytes 9961472 | tf_op jit(solution)/shard_map/dot_general | solution.py:181
  249.7 12.3 %copy.125 = bf16[2048,2048]{1,0:T(8,128)(2,1)} copy(bf16[2048,2048]{0,1:T(8,128)(2,1)} %convert_bitcast_fusion) | data formatting | bytes 16777216
  262.7 76.5 %all-reduce = (f32[2048]{0:T(1024)}, f32[2048]{0:T(1024)}) all-reduce(f32[2048]{0:T(1024)S(1)} %get-tuple-element.41, f32[2048]{0:T(1024)S(1)} %copy-done.18), channel_id=1, replica_groups=mesh['dp'=16,'tensor'=8] {'dp'}, use_global_device_ids=true, to_apply=%region_10.12 | all-reduce | flops 4096 | bytes 32768 | tf_op jit(solution)/shard_map/psum | solution.py:188
  341.1 7.7 %reduce-scatter.7.cloned.1.call-done = bf16[128,2048]{1,0:T(8,128)(2,1)} async-done(((bf16[2048,2048]{1,0:T(8,128)(2,1)}), bf16[128,2048]{1,0:T(8,128)(2,1)}) %reduce-scatter.7.cloned.1.call-update) | async-done | bytes 524304
  (197 shorter events, 99.6 us)
Async XLA Ops:
  7.2 130.6 %all-gather.2.cloned.1.call-start = ((), (), s32[]{:S(2)}) async-start(), calls=%async_computation.3 | async-start | bytes 5570560 | tf_op jit(solution)/shard_map/all_gather | solution.py:130
  7.9 331.3 %reduce-scatter.5.cloned.1.call-start = ((), (), s32[]{:S(2)}) async-start(), calls=%async_computation.4 | async-start | bytes 5570560 | tf_op jit(solution)/shard_map/reduce_scatter | solution.py:172
  16.3 12.7 %collective-permute-start = (bf16[96,4096]{1,0:T(8,128)(2,1)S(1)}, bf16[96,4096]{1,0:T(8,128)(2,1)}, u32[]{:S(2)}, u32[]{:S(2)}) collective-permute-start(bf16[96,4096]{1,0:T(8,128)(2,1)S(1)} %get-tuple-element.59), channel_id=1, source_target_pairs={{0,1},{1,2},{2,3},{3,4},{4,5},{5,6},{6,7},{7,0},{8,9},{9,10},{10,1... | collective-permute-start | bytes 2359304 | tf_op jit(solution)/shard_map/ppermute | solution.py:73
  16.3 12.7 %collective-permute-start.7 = (bf16[96,4096]{1,0:T(8,128)(2,1)S(1)}, bf16[96,4096]{1,0:T(8,128)(2,1)}, u32[]{:S(2)}, u32[]{:S(2)}) collective-permute-start(bf16[96,4096]{1,0:T(8,128)(2,1)S(1)} %get-tuple-element.58), channel_id=1, source_target_pairs={{0,7},{1,0},{2,1},{3,2},{4,3},{5,4},{6,5},{7,6},{8,15},{9,8},{10,9... | collective-permute-start | bytes 2359304 | tf_op jit(solution)/shard_map/ppermute | solution.py:74
  29.0 12.9 %collective-permute-start.1 = (bf16[96,4096]{1,0:T(8,128)(2,1)}, bf16[96,4096]{1,0:T(8,128)(2,1)}, u32[]{:S(2)}, u32[]{:S(2)}) collective-permute-start(bf16[96,4096]{1,0:T(8,128)(2,1)} %collective-permute-done), channel_id=1, source_target_pairs={{0,1},{1,2},{2,3},{3,4},{4,5},{5,6},{6,7},{7,0},{8,9},{9,10},{10,1... | collective-permute-start | bytes 2359304 | tf_op jit(solution)/shard_map/ppermute | solution.py:73
  29.1 12.9 %collective-permute-start.8 = (bf16[96,4096]{1,0:T(8,128)(2,1)}, bf16[96,4096]{1,0:T(8,128)(2,1)}, u32[]{:S(2)}, u32[]{:S(2)}) collective-permute-start(bf16[96,4096]{1,0:T(8,128)(2,1)} %collective-permute-done.7), channel_id=1, source_target_pairs={{0,7},{1,0},{2,1},{3,2},{4,3},{5,4},{6,5},{7,6},{8,15},{9,8},{10,9... | collective-permute-start | bytes 2359304 | tf_op jit(solution)/shard_map/ppermute | solution.py:74
  42.0 12.8 %collective-permute-start.2 = (bf16[96,4096]{1,0:T(8,128)(2,1)}, bf16[96,4096]{1,0:T(8,128)(2,1)S(1)}, u32[]{:S(2)}, u32[]{:S(2)}) collective-permute-start(bf16[96,4096]{1,0:T(8,128)(2,1)} %collective-permute-done.1), channel_id=1, source_target_pairs={{0,1},{1,2},{2,3},{3,4},{4,5},{5,6},{6,7},{7,0},{8,9},{9,10},{10,1... | collective-permute-start | bytes 2359304 | tf_op jit(solution)/shard_map/ppermute | solution.py:73
  42.0 12.8 %collective-permute-start.9 = (bf16[96,4096]{1,0:T(8,128)(2,1)}, bf16[96,4096]{1,0:T(8,128)(2,1)S(1)}, u32[]{:S(2)}, u32[]{:S(2)}) collective-permute-start(bf16[96,4096]{1,0:T(8,128)(2,1)} %collective-permute-done.8), channel_id=1, source_target_pairs={{0,7},{1,0},{2,1},{3,2},{4,3},{5,4},{6,5},{7,6},{8,15},{9,8},{10,9... | collective-permute-start | bytes 2359304 | tf_op jit(solution)/shard_map/ppermute | solution.py:74
  54.8 12.6 %collective-permute-start.3 = (bf16[96,4096]{1,0:T(8,128)(2,1)S(1)}, bf16[96,4096]{1,0:T(8,128)(2,1)S(1)}, u32[]{:S(2)}, u32[]{:S(2)}) collective-permute-start(bf16[96,4096]{1,0:T(8,128)(2,1)S(1)} %collective-permute-done.2), channel_id=1, source_target_pairs={{0,1},{1,2},{2,3},{3,4},{4,5},{5,6},{6,7},{7,0},{8,9},{9,10},{10,1... | collective-permute-start | bytes 2359304 | tf_op jit(solution)/shard_map/ppermute | solution.py:73
  54.8 12.9 %collective-permute-start.10 = (bf16[96,4096]{1,0:T(8,128)(2,1)S(1)}, bf16[96,4096]{1,0:T(8,128)(2,1)S(1)}, u32[]{:S(2)}, u32[]{:S(2)}) collective-permute-start(bf16[96,4096]{1,0:T(8,128)(2,1)S(1)} %collective-permute-done.9), channel_id=1, source_target_pairs={{0,7},{1,0},{2,1},{3,2},{4,3},{5,4},{6,5},{7,6},{8,15},{9,8},{10,9... | collective-permute-start | bytes 2359304 | tf_op jit(solution)/shard_map/ppermute | solution.py:74
  67.5 12.6 %collective-permute-start.4 = (bf16[96,4096]{1,0:T(8,128)(2,1)S(1)}, bf16[96,4096]{1,0:T(8,128)(2,1)S(1)}, u32[]{:S(2)}, u32[]{:S(2)}) collective-permute-start(bf16[96,4096]{1,0:T(8,128)(2,1)S(1)} %collective-permute-done.3), channel_id=1, source_target_pairs={{0,1},{1,2},{2,3},{3,4},{4,5},{5,6},{6,7},{7,0},{8,9},{9,10},{10,1... | collective-permute-start | bytes 2359304 | tf_op jit(solution)/shard_map/ppermute | solution.py:73
  67.7 13.0 %collective-permute-start.11 = (bf16[96,4096]{1,0:T(8,128)(2,1)S(1)}, bf16[96,4096]{1,0:T(8,128)(2,1)S(1)}, u32[]{:S(2)}, u32[]{:S(2)}) collective-permute-start(bf16[96,4096]{1,0:T(8,128)(2,1)S(1)} %collective-permute-done.10), channel_id=1, source_target_pairs={{0,7},{1,0},{2,1},{3,2},{4,3},{5,4},{6,5},{7,6},{8,15},{9,8},{10,9... | collective-permute-start | bytes 2359304 | tf_op jit(solution)/shard_map/ppermute | solution.py:74
  80.1 12.6 %collective-permute-start.5 = (bf16[96,4096]{1,0:T(8,128)(2,1)S(1)}, bf16[96,4096]{1,0:T(8,128)(2,1)S(1)}, u32[]{:S(2)}, u32[]{:S(2)}) collective-permute-start(bf16[96,4096]{1,0:T(8,128)(2,1)S(1)} %collective-permute-done.4), channel_id=1, source_target_pairs={{0,1},{1,2},{2,3},{3,4},{4,5},{5,6},{6,7},{7,0},{8,9},{9,10},{10,1... | collective-permute-start | bytes 2359304 | tf_op jit(solution)/shard_map/ppermute | solution.py:73
  80.7 12.6 %collective-permute-start.12 = (bf16[96,4096]{1,0:T(8,128)(2,1)S(1)}, bf16[96,4096]{1,0:T(8,128)(2,1)S(1)}, u32[]{:S(2)}, u32[]{:S(2)}) collective-permute-start(bf16[96,4096]{1,0:T(8,128)(2,1)S(1)} %collective-permute-done.11), channel_id=1, source_target_pairs={{0,7},{1,0},{2,1},{3,2},{4,3},{5,4},{6,5},{7,6},{8,15},{9,8},{10,9... | collective-permute-start | bytes 2359304 | tf_op jit(solution)/shard_map/ppermute | solution.py:74
  92.7 12.6 %collective-permute-start.6 = (bf16[96,4096]{1,0:T(8,128)(2,1)S(1)}, bf16[96,4096]{1,0:T(8,128)(2,1)S(1)}, u32[]{:S(2)}, u32[]{:S(2)}) collective-permute-start(bf16[96,4096]{1,0:T(8,128)(2,1)S(1)} %collective-permute-done.5), channel_id=1, source_target_pairs={{0,1},{1,2},{2,3},{3,4},{4,5},{5,6},{6,7},{7,0},{8,9},{9,10},{10,1... | collective-permute-start | bytes 2359304 | tf_op jit(solution)/shard_map/ppermute | solution.py:73
  93.3 12.6 %collective-permute-start.13 = (bf16[96,4096]{1,0:T(8,128)(2,1)S(1)}, bf16[96,4096]{1,0:T(8,128)(2,1)S(1)}, u32[]{:S(2)}, u32[]{:S(2)}) collective-permute-start(bf16[96,4096]{1,0:T(8,128)(2,1)S(1)} %collective-permute-done.12), channel_id=1, source_target_pairs={{0,7},{1,0},{2,1},{3,2},{4,3},{5,4},{6,5},{7,6},{8,15},{9,8},{10,9... | collective-permute-start | bytes 2359304 | tf_op jit(solution)/shard_map/ppermute | solution.py:74
  148.5 89.0 %all-to-all-start = ((bf16[8,384,512]{2,1,0:T(8,128)(2,1)}), bf16[8,384,512]{2,1,0:T(8,128)(2,1)}, u32[]{:S(2)}, u32[]{:S(2)}) async-start(bf16[8,384,512]{2,1,0:T(8,128)(2,1)} %bitcast.163), calls=%async_computation | async-start | bytes 6291456 | tf_op jit(solution)/shard_map/all_to_all | solution.py:137
  153.1 195.7 %reduce-scatter.7.cloned.1.call-start = ((), (), s32[]{:S(2)}) async-start(), calls=%async_computation.5 | async-start | bytes 8912896
  165.7 33.2 %collective-permute-start.15 = (bf16[1,384,512]{2,1,0:T(8,128)(2,1)}, bf16[1,384,512]{2,1,0:T(8,128)(2,1)S(1)}, u32[]{:S(2)}, u32[]{:S(2)}) collective-permute-start(bf16[1,384,512]{2,1,0:T(8,128)(2,1)} %get-tuple-element.54), channel_id=1, source_target_pairs={{0,2},{1,3},{2,0},{3,1},{4,6},{5,7},{6,4},{7,5},{8,10},{9,11},{10,... | collective-permute-start | bytes 1179656 | tf_op jit(solution)/shard_map/ppermute | solution.py:165
  167.7 38.7 %collective-permute-start.16 = (bf16[1,384,512]{2,1,0:T(8,128)(2,1)}, bf16[1,384,512]{2,1,0:T(8,128)(2,1)S(1)}, u32[]{:S(2)}, u32[]{:S(2)}) collective-permute-start(bf16[1,384,512]{2,1,0:T(8,128)(2,1)} %get-tuple-element.53), channel_id=1, source_target_pairs={{0,3},{1,2},{2,1},{3,0},{4,7},{5,6},{6,5},{7,4},{8,11},{9,10},{10,... | collective-permute-start | bytes 1179656 | tf_op jit(solution)/shard_map/ppermute | solution.py:165
  167.8 49.6 %collective-permute-start.17 = (bf16[1,384,512]{2,1,0:T(8,128)(2,1)}, bf16[1,384,512]{2,1,0:T(8,128)(2,1)S(1)}, u32[]{:S(2)}, u32[]{:S(2)}) collective-permute-start(bf16[1,384,512]{2,1,0:T(8,128)(2,1)} %get-tuple-element.52), channel_id=1, source_target_pairs={{0,4},{1,5},{2,6},{3,7},{4,0},{5,1},{6,2},{7,3},{8,12},{9,13},{10,... | collective-permute-start | bytes 1179656 | tf_op jit(solution)/shard_map/ppermute | solution.py:165
  170.8 54.1 %collective-permute-start.18 = (bf16[1,384,512]{2,1,0:T(8,128)(2,1)}, bf16[1,384,512]{2,1,0:T(8,128)(2,1)S(1)}, u32[]{:S(2)}, u32[]{:S(2)}) collective-permute-start(bf16[1,384,512]{2,1,0:T(8,128)(2,1)} %get-tuple-element.51), channel_id=1, source_target_pairs={{0,5},{1,4},{2,7},{3,6},{4,1},{5,0},{6,3},{7,2},{8,13},{9,12},{10,... | collective-permute-start | bytes 1179656 | tf_op jit(solution)/shard_map/ppermute | solution.py:165
  171.1 54.5 %collective-permute-start.19 = (bf16[1,384,512]{2,1,0:T(8,128)(2,1)}, bf16[1,384,512]{2,1,0:T(8,128)(2,1)S(1)}, u32[]{:S(2)}, u32[]{:S(2)}) collective-permute-start(bf16[1,384,512]{2,1,0:T(8,128)(2,1)} %get-tuple-element.50), channel_id=1, source_target_pairs={{0,6},{1,7},{2,4},{3,5},{4,2},{5,3},{6,0},{7,1},{8,14},{9,15},{10,... | collective-permute-start | bytes 1179656 | tf_op jit(solution)/shard_map/ppermute | solution.py:165
  198.9 29.1 %collective-permute-start.20 = (bf16[1,384,512]{2,1,0:T(8,128)(2,1)}, bf16[1,384,512]{2,1,0:T(8,128)(2,1)S(1)}, u32[]{:S(2)}, u32[]{:S(2)}) collective-permute-start(bf16[1,384,512]{2,1,0:T(8,128)(2,1)} %get-tuple-element.49), channel_id=1, source_target_pairs={{0,7},{1,6},{2,5},{3,4},{4,3},{5,2},{6,1},{7,0},{8,15},{9,14},{10,... | collective-permute-start | bytes 1179656 | tf_op jit(solution)/shard_map/ppermute | solution.py:165
  (28 other events, 175.3 us)
Sparse Core Ops, SparseCore 0:
  10.2 58.9 all-gather.1
  132.3 81.8 reduce-scatter.4
  262.2 86.6 reduce-scatter.6
